TPU v7x, 32 devices: a whole 2x2x4 slice. The times are simulated.
32 devices in a mesh: teacher: 4 (over y, x), vocab: 8 (over z, core).
Axes of the slice: x: 2, y: 2, z: 4, core: 2. Of those that a mesh axis runs over, the one named last changes fastest.
Arguments:
- teacher_hidden: bfloat16 [4, 1024, 4096], P('teacher', 'vocab'), may hold values from -180 to 180
- teacher_head: bfloat16 [4, 4096, 32000], P('teacher', None, 'vocab'), may hold values from -0.375 to 0.375
- student_hidden: bfloat16 [1024, 4096], P('teacher'), may hold values from -180 to 180
- student_head: bfloat16 [4096, 32000], P('teacher', 'vocab'), may hold values from -0.375 to 0.375
Outputs:
- loss: float32 [], replicated
- grad_hidden: float32 [1024, 4096], P('teacher', 'vocab')
- grad_weight: float32 [4096, 32000], P('teacher', 'vocab')
All inputs are finite; a program needn't handle non-finite values.
Results may differ from a plain program's by a relative error of at most 0.0027.
Values may be sent and summed in bfloat16 or wider, within the bound.
A program may use at most 192 MiB of HBM per device.

v0:
```python
import jax
import jax.numpy as jnp
from jax import lax
from jax.sharding import PartitionSpec as P

TOK = 1024


def teacher_stats(logits):
    local_top = jnp.max(logits, axis=-1)
    top = lax.pmax(local_top, "vocab")
    shifted = jnp.exp(logits - top[:, None])
    total, moment = lax.psum(
        (jnp.sum(shifted, axis=-1), jnp.sum(shifted * logits, axis=-1)), "vocab"
    )
    return (top, total, moment)


def paired_lse(stacked):
    local_top = jnp.max(stacked, axis=-1)
    top = lax.pmax(local_top, "vocab")
    total = lax.psum(jnp.sum(jnp.exp(stacked - top[..., None]), axis=-1), "vocab")
    return top + jnp.log(total)


def per_device(teacher_hidden, teacher_head, student_hidden, student_head):
    head = teacher_head[0]
    logits = jnp.dot(
        lax.all_gather(teacher_hidden[0], "vocab", axis=0, tiled=True),
        head,
        preferred_element_type=jnp.float32,
    )
    top, total, moment = teacher_stats(logits)
    lse = top + jnp.log(total)
    entropy = lse - moment / total
    confid = jnp.exp(-entropy)
    weighted = confid[:, None] * (logits - lse[:, None])
    wsum, csum = (
        lax.psum_scatter(weighted, "teacher", scatter_dimension=0, tiled=True),
        lax.psum_scatter(confid, "teacher", scatter_dimension=0, tiled=True),
    )
    raw = wsum / csum[:, None]
    full_head = lax.all_gather(student_head, "teacher", axis=0, tiled=True)
    slog = jnp.dot(student_hidden, full_head, preferred_element_type=jnp.float32)
    both_lse = paired_lse(jnp.stack([raw, slog]))
    target = raw - both_lse[0][:, None]
    slp = slog - both_lse[1][:, None]
    probs = jnp.exp(target)
    partial_kl = jnp.sum(probs * (target - slp))
    loss = lax.psum(partial_kl, ("teacher", "vocab")) / TOK
    gradl = (jnp.exp(slp) - probs).astype(jnp.bfloat16)
    grad_hidden = lax.psum_scatter(
        lax.dot_general(
            full_head, gradl, (((1,), (1,)), ((), ())), preferred_element_type=jnp.float32
        ),
        "vocab",
        scatter_dimension=0,
        tiled=True,
    ).T
    columns = lax.all_to_all(student_hidden, "teacher", split_axis=1, concat_axis=0, tiled=True)
    all_grads = lax.all_gather(gradl, "teacher", axis=0, tiled=True)
    grad_weight = lax.dot_general(
        columns, all_grads, (((0,), (0,)), ((), ())), preferred_element_type=jnp.float32
    )
    return (loss, grad_hidden, grad_weight)


def solution(mesh):
    placed = (
        P("teacher", "vocab", None),
        P("teacher", None, "vocab"),
        P("teacher", None),
        P("teacher", "vocab"),
    )
    return jax.shard_map(
        per_device,
        mesh=mesh,
        in_specs=placed,
        out_specs=(P(), P("teacher", "vocab"), P("teacher", "vocab")),
        check_vma=False,
    )
```

profile of v0, /device:TPU:0, one launch (start us, length us, event | category | flops | bytes accessed | tf_op | source)
XLA Modules:
  0.0 849.6 jit_solution(5529223192047300215)
XLA Ops:
  7.9 86.4 %all-gather.9.cloned.1.call-done = bf16[1,1024,4096]{2,1,0:T(8,128)(2,1)} async-done(((bf16[1,128,4096]{2,1,0:T(8,128)(2,1)}), bf16[1,1024,4096]{2,1,0:T(8,128)(2,1)}) %all-gather.9.cloned.1.call-update) | async-done | bytes 8388624 | tf_op jit(solution)/shard_map/all_gather | solution.py:29
  94.4 41.8 %fusion.7 = (f32[1024]{0:T(1024)S(1)}, f32[1024,4000]{0,1:T(8,128)}) fusion(bf16[1,4096,4000]{1,2,0:T(8,128)(2,1)} %param.5, bf16[1,1024,4096]{2,1,0:T(8,128)(2,1)} %all-gather.9.cloned.1.call-done), kind=kOutput, calls=%fused_computation.20 | convolution fusion | flops 33558528000 | bytes 57544704 | tf_op jit(solution)/shard_map/dot_general | solution.py:28
  136.2 14.0 %pmax.14 = f32[1024]{0:T(1024)S(1)} all-reduce(f32[1024]{0:T(1024)S(1)} %get-tuple-element.13), channel_id=1, replica_groups=mesh['teacher'=4,'vocab'=8] {'vocab'}, use_global_device_ids=true, to_apply=%region_1.0 | all-reduce | flops 1024 | bytes 8192 | tf_op jit(solution)/shard_map/pmax | solution.py:11
  150.2 7.6 multiply_reduce_fusion
  157.8 13.9 %all-reduce.1 = (f32[1024]{0:T(1024)S(1)}, f32[1024]{0:T(1024)S(1)}) all-reduce(f32[1024]{0:T(1024)S(1)} %get-tuple-element.4, f32[1024]{0:T(1024)S(1)} %get-tuple-element.3), channel_id=1, replica_groups=mesh['teacher'=4,'vocab'=8] {'vocab'}, use_global_device_ids=true, to_apply=%region_3.0 | all-reduce | flops 2048 | bytes 16384 | tf_op jit(solution)/shard_map/psum | solution.py:13
  171.7 11.5 %subtract_multiply_fusion = f32[1024,4000]{0,1:T(8,128)} fusion(f32[1024,4000]{0,1:T(8,128)} %get-tuple-element.14, f32[1024]{0:T(1024)S(1)} %get-tuple-element.10, f32[1024]{0:T(1024)S(1)} %get-tuple-element.9), kind=kLoop, calls=%fused_computation.2 | loop fusion | flops 8192000 | bytes 32776192 | tf_op jit(solution)/shard_map/mul | solution.py:37
  185.3 10.4 %all-reduce = f32[1024]{0:T(1024)S(1)} all-reduce(f32[1024]{0:T(1024)S(1)} %get-tuple-element.9), channel_id=4, replica_groups=mesh['teacher'=4,'vocab'=8] {'teacher'}, use_global_device_ids=true, to_apply=%region_7.0.clone | all-reduce | flops 1024 | bytes 8192
  195.8 136.6 %reduce-scatter.3.cloned.1.call-done = f32[256,4000]{0,1:T(8,128)} async-done(((f32[1024,4000]{0,1:T(8,128)}), f32[256,4000]{0,1:T(8,128)}) %reduce-scatter.3.cloned.1.call-update) | async-done | bytes 4096016 | tf_op jit(solution)/shard_map/reduce_scatter | solution.py:39
  332.4 4.4 fusion.5
  336.8 288.4 %all-gather.5.cloned.1.call-done = bf16[4096,4000]{0,1:T(8,128)(2,1)} async-done(((bf16[1024,4000]{0,1:T(8,128)(2,1)}), bf16[4096,4000]{0,1:T(8,128)(2,1)}) %all-gather.5.cloned.1.call-update) | async-done | bytes 32768016 | tf_op jit(solution)/shard_map/all_gather | solution.py:43
  625.1 14.1 %fusion.8 = f32[256,4000]{0,1:T(8,128)S(1)} fusion(bf16[256,4096]{1,0:T(8,128)(2,1)S(1)} %copy-done.2, bf16[4096,4000]{0,1:T(8,128)(2,1)} %all-gather.5.cloned.1.call-done), kind=kOutput, calls=%fused_computation.21 | convolution fusion | flops 8388608000 | bytes 38961152 | tf_op jit(solution)/shard_map/dot_general | solution.py:44
  639.3 2.0 copy-done.1
  641.8 16.3 %pmax.15 = f32[2,256]{1,0:T(2,128)S(1)} all-reduce(f32[2,256]{1,0:T(2,128)S(1)} %fusion.4), channel_id=1, replica_groups=mesh['teacher'=4,'vocab'=8] {'vocab'}, use_global_device_ids=true, to_apply=%region_9.0 | all-reduce | flops 512 | bytes 4096 | tf_op jit(solution)/shard_map/pmax | solution.py:21
  658.2 4.0 exponential_reduce_fusion
  662.1 13.8 %psum.30 = f32[2,256]{1,0:T(2,128)S(1)} all-reduce(f32[2,256]{1,0:T(2,128)S(1)} %exponential_reduce_fusion), channel_id=1, replica_groups=mesh['teacher'=4,'vocab'=8] {'vocab'}, use_global_device_ids=true, to_apply=%region_11.0 | all-reduce | flops 512 | bytes 4096 | tf_op jit(solution)/shard_map/psum | solution.py:22
  675.9 6.9 subtract_convert_fusion
  682.9 18.8 %convolution_bitcast_fusion.1 = f32[4096,256]{0,1:T(8,128)} fusion(bf16[256,4000]{0,1:T(8,128)(2,1)} %get-tuple-element.7, bf16[4096,4000]{0,1:T(8,128)(2,1)} %all-gather.5.cloned.1.call-done), kind=kOutput, calls=%fused_computation.11 | convolution fusion | flops 8388608000 | bytes 39010304 | tf_op jit(solution)/shard_map/dot_general | solution.py:53
  701.8 2.5 copy.9
  704.2 32.7 %all_to_all.19 = bf16[256,4,1024]{0,2,1:T(8,128)(2,1)S(1)} all-to-all(bf16[256,4,1024]{0,2,1:T(8,128)(2,1)} %bitcast.33), channel_id=1, replica_groups=mesh['teacher'=4,'vocab'=8] {'teacher'}, dimensions={1} | all-to-all | bytes 4194304 | tf_op jit(solution)/shard_map/all_to_all | solution.py:60
  736.9 2.5 copy.10
  739.4 40.0 %psum.31 = f32[]{:T(128)} all-reduce(f32[]{:T(128)} %get-tuple-element.8), channel_id=1, replica_groups=mesh['teacher'=4,'vocab'=8] {'teacher','vocab'}, use_global_device_ids=true, to_apply=%region_13.0 | all-reduce | flops 1 | bytes 8 | tf_op jit(solution)/shard_map/psum | solution.py:50
  780.0 9.0 %all-gather.7.cloned.1.call-done = bf16[1024,4000]{0,1:T(8,128)(2,1)} async-done(((bf16[256,4000]{0,1:T(8,128)(2,1)}), bf16[1024,4000]{0,1:T(8,128)(2,1)}) %all-gather.7.cloned.1.call-update) | async-done | bytes 8192016 | tf_op jit(solution)/shard_map/all_gather | solution.py:61
  789.1 15.9 %convolution_bitcast_fusion = f32[1024,4000]{0,1:T(8,128)} fusion(bf16[1024,4000]{0,1:T(8,128)(2,1)} %all-gather.7.cloned.1.call-done, bf16[1024,1024]{1,0:T(8,128)(2,1)} %bitcast.34), kind=kOutput, calls=%fused_computation.6 | convolution fusion | flops 8388608000 | bytes 26673152 | tf_op jit(solution)/shard_map/dot_general | solution.py:62
  804.9 37.0 %reduce-scatter.5.cloned.1.call-done = f32[512,256]{0,1:T(8,128)} async-done(((f32[4096,256]{0,1:T(8,128)}), f32[512,256]{0,1:T(8,128)}) %reduce-scatter.5.cloned.1.call-update) | async-done | bytes 524304 | tf_op jit(solution)/shard_map/reduce_scatter | solution.py:52
  (23 shorter events, 2.9 us)
Async XLA Ops:
  7.2 87.2 %all-gather.9.cloned.1.call-start = ((), (), s32[]{:S(2)}) async-start(), calls=%async_computation.7 | async-start | bytes 9437184 | tf_op jit(solution)/shard_map/all_gather | solution.py:29
  7.9 324.5 %reduce-scatter.3.cloned.1.call-start = ((), (), s32[]{:S(2)}) async-start(), calls=%async_computation.3 | async-start | bytes 20480000 | tf_op jit(solution)/shard_map/reduce_scatter | solution.py:39
  183.3 0.8 copy-start.3
  183.3 441.8 %copy-start.2 = (bf16[256,4096]{1,0:T(8,128)(2,1)S(1)}, bf16[256,4096]{1,0:T(8,128)(2,1)}, u32[]{:S(2)}) copy-start(bf16[256,4096]{1,0:T(8,128)(2,1)} %param.6) | copy-start | bytes 6291460
  183.3 441.8 %all-gather.5.cloned.1.call-start = ((), (), s32[]{:S(2)}) async-start(), calls=%async_computation.4 | async-start | bytes 40960000 | tf_op jit(solution)/shard_map/all_gather | solution.py:43
  184.0 605.0 %all-gather.7.cloned.1.call-start = ((), (), s32[]{:S(2)}) async-start(), calls=%async_computation.6 | async-start | bytes 10240000 | tf_op jit(solution)/shard_map/all_gather | solution.py:61
  625.1 16.1 %copy-start = (f32[1,256,4000]{1,2,0:T(8,128)S(1)}, f32[1,256,4000]{1,2,0:T(8,128)}, u32[]{:S(2)}) copy-start(f32[1,256,4000]{1,2,0:T(8,128)} %fusion.5) | copy-start | bytes 12288004
  639.3 2.0 copy-start.1
  682.9 159.0 %reduce-scatter.5.cloned.1.call-start = ((), (), s32[]{:S(2)}) async-start(), calls=%async_computation.5 | async-start | bytes 4718592 | tf_op jit(solution)/shard_map/reduce_scatter | solution.py:52
Sparse Core Ops, SparseCore 0:
  9.6 84.7 all-gather.8
  183.4 148.9 reduce-scatter.2
  334.4 290.6 all-gather.4
  683.0 106.0 all-gather.6
  791.9 49.9 reduce-scatter.4
where the time goes:
time: 850 us
  waiting for transfers between devices  559 us (66%)
  blocking collectives  141 us (17%)
  matrix products  90.6 us (11%)
  other arithmetic  34.9 us (4%)
  between operations  16.3 us (2%)
    all_gather x1, waiting for transfers between devices, per_device(): full_head = lax.all_gather(student_head, 'teacher', axis=0, tiled=True)  288 us
    reduce_scatter x1, waiting for transfers between devices, per_device(): lax.psum_scatter(weighted, 'teacher', scatter_dimension=0, tiled=True)  137 us
    all_gather x1, waiting for transfers between devices, per_device(): lax.all_gather(teacher_hidden[0], 'vocab', axis=0, tiled=True)  86.4 us
    dot_general x1, matrix products, per_device(): jnp.dot(lax.all_gather(teacher_hidden[0], 'vocab', axis=0, tiled=True), h...  41.8 us
    psum x1, blocking collectives, per_device(): loss = lax.psum(partial_kl, ('teacher', 'vocab')) / TOK  40 us
    reduce_scatter x1, waiting for transfers between devices, per_device(): lax.psum_scatter(lax.dot_general(full_head, gradl, (((1,), (1,)), ((), ()...  37 us
    all_to_all x1, blocking collectives, per_device(): lax.all_to_all(student_hidden, 'teacher', split_axis=1, concat_axis=0, ti...  32.7 us
    dot_general x1, matrix products, per_device(): lax.dot_general(full_head, gradl, (((1,), (1,)), ((), ())), preferred_ele...  18.8 us
  transfers between devices with their start and end apart: 5, of which 5 were waited for; matrix products, arithmetic and copies ran while one was open for 5% of the time, Pallas kernels for 0%

commit v1 on v0

--- a/solution.py
+++ b/solution.py
@@ -40,7 +40,14 @@
         lax.psum_scatter(confid, "teacher", scatter_dimension=0, tiled=True),
     )
     raw = wsum / csum[:, None]
-    full_head = lax.all_gather(student_head, "teacher", axis=0, tiled=True)
+    ring = [student_head]
+    for hop in range(3):
+        ring.append(lax.ppermute(ring[-1], "teacher", [(dev, (dev + 1) % 4) for dev in range(4)]))
+    full_head = jnp.roll(
+        jnp.concatenate(ring[::-1], axis=0),
+        (lax.axis_index("teacher") + 1) * ring[0].shape[0],
+        axis=0,
+    )
     slog = jnp.dot(student_hidden, full_head, preferred_element_type=jnp.float32)
     both_lse = paired_lse(jnp.stack([raw, slog]))
     target = raw - both_lse[0][:, None]

time: 850 us -> 1140 us (1.34)
  blocking collectives: 141 us -> 300 us
  waiting for transfers between devices: 559 us -> 632 us
  local copies, waits for them, and re-layouts: 7.62 us -> 67.7 us
    ppermute x0 -> x3, waiting for transfers between devices: none -> 486 us  [per_device(): lax.ppermute(ring[-1], 'teacher', [(dev, (dev + 1) % 4) for dev in range(...]
    all_gather x1 -> x0, waiting for transfers between devices: 288 us -> none  [per_device(): full_head = lax.all_gather(student_head, 'teacher', axis=0, tiled=True)]
    unnamed x1, blocking collectives: 10.4 us -> 178 us
    reduce_scatter x1, waiting for transfers between devices: 137 us -> 0.01 us  [per_device(): lax.psum_scatter(weighted, 'teacher', scatter_dimension=0, tiled=True)]
    unnamed x11 -> x25, local copies, waits for them, and re-layouts: 5.11 us -> 61.1 us
    all_gather x1, waiting for transfers between devices: 9.04 us -> 58.4 us  [per_device(): all_grads = lax.all_gather(gradl, 'teacher', axis=0, tiled=True)]
    reduce_scatter x1, waiting for transfers between devices: 37 us -> 0.02 us  [per_device(): lax.psum_scatter(lax.dot_general(full_head, gradl, (((1,), (1,)), ((), ()...]
  transfers between devices with their start and end apart: 5 -> 7, of which waited for: 5 -> 4; matrix products, arithmetic and copies ran while one was open for 5% -> 7% of each run, Pallas kernels for 0% -> 0%
where the time goes in v1:
time: 1140 us
  waiting for transfers between devices  632 us (55%)
  blocking collectives  300 us (26%)
  matrix products  92.9 us (8%)
  local copies, waits for them, and re-layouts  67.7 us (6%)
  other arithmetic  31.8 us (3%)
  between operations  16.3 us (1%)
    ppermute x3, waiting for transfers between devices, per_device(): lax.ppermute(ring[-1], 'teacher', [(dev, (dev + 1) % 4) for dev in range(...  486 us
    unnamed x1, blocking collectives  178 us
    all_gather x1, waiting for transfers between devices, per_device(): lax.all_gather(teacher_hidden[0], 'vocab', axis=0, tiled=True)  86.4 us
    unnamed x25, local copies, waits for them, and re-layouts  61.1 us
    all_gather x1, waiting for transfers between devices, per_device(): all_grads = lax.all_gather(gradl, 'teacher', axis=0, tiled=True)  58.4 us
    dot_general x1, matrix products, per_device(): jnp.dot(lax.all_gather(teacher_hidden[0], 'vocab', axis=0, tiled=True), h...  41.8 us
    psum x1, blocking collectives, per_device(): loss = lax.psum(partial_kl, ('teacher', 'vocab')) / TOK  37.6 us
    all_to_all x1, blocking collectives, per_device(): lax.all_to_all(student_hidden, 'teacher', split_axis=1, concat_axis=0, ti...  29 us
  transfers between devices with their start and end apart: 7, of which 4 were waited for; matrix products, arithmetic and copies ran while one was open for 7% of the time, Pallas kernels for 0%

profile of v1, /device:TPU:0, one launch (start us, length us, event | category | flops | bytes accessed | tf_op | source)
XLA Modules:
  0.0 1144.0 jit_solution(2261004604023277859)
XLA Ops:
  7.9 86.4 %all-gather.6.cloned.1.call-done = bf16[1,1024,4096]{2,1,0:T(8,128)(2,1)} async-done(((bf16[1,128,4096]{2,1,0:T(8,128)(2,1)}), bf16[1,1024,4096]{2,1,0:T(8,128)(2,1)}) %all-gather.6.cloned.1.call-update) | async-done | bytes 8388624 | tf_op jit(solution)/shard_map/all_gather | solution.py:29
  94.4 41.8 %fusion.13 = (f32[1024]{0:T(1024)S(1)}, f32[1024,4000]{0,1:T(8,128)}) fusion(bf16[1,4096,4000]{1,2,0:T(8,128)(2,1)} %param.5, bf16[1,1024,4096]{2,1,0:T(8,128)(2,1)} %all-gather.6.cloned.1.call-done), kind=kOutput, calls=%fused_computation.34 | convolution fusion | flops 33558528000 | bytes 57544704 | tf_op jit(solution)/shard_map/dot_general | solution.py:28
  136.2 14.0 %pmax.14 = f32[1024]{0:T(1024)S(1)} all-reduce(f32[1024]{0:T(1024)S(1)} %get-tuple-element.25), channel_id=1, replica_groups=mesh['teacher'=4,'vocab'=8] {'vocab'}, use_global_device_ids=true, to_apply=%region_1.0 | all-reduce | flops 1024 | bytes 8192 | tf_op jit(solution)/shard_map/pmax | solution.py:11
  150.2 7.6 multiply_reduce_fusion
  157.8 13.9 %all-reduce.1 = (f32[1024]{0:T(1024)S(1)}, f32[1024]{0:T(1024)S(1)}) all-reduce(f32[1024]{0:T(1024)S(1)} %get-tuple-element.16, f32[1024]{0:T(1024)S(1)} %get-tuple-element.15), channel_id=1, replica_groups=mesh['teacher'=4,'vocab'=8] {'vocab'}, use_global_device_ids=true, to_apply=%region_3.0 | all-reduce | flops 2048 | bytes 16384 | tf_op jit(solution)/shard_map/psum | solution.py:13
  171.7 11.5 %subtract_multiply_fusion = f32[1024,4000]{0,1:T(8,128)} fusion(f32[1024,4000]{0,1:T(8,128)} %get-tuple-element.26, f32[1024]{0:T(1024)S(1)} %get-tuple-element.22, f32[1024]{0:T(1024)S(1)} %get-tuple-element.21), kind=kLoop, calls=%fused_computation.6 | loop fusion | flops 8192000 | bytes 32776192 | tf_op jit(solution)/shard_map/mul | solution.py:37
  185.1 309.0 %collective-permute-done = bf16[1024,4000]{0,1:T(8,128)(2,1)S(1)} collective-permute-done((bf16[1024,4000]{0,1:T(8,128)(2,1)}, bf16[1024,4000]{0,1:T(8,128)(2,1)S(1)}, u32[]{:S(2)}, u32[]{:S(2)}) %collective-permute-start) | collective-permute-done | bytes 8192032 | tf_op jit(solution)/shard_map/ppermute | solution.py:45
  498.1 177.2 %collective-permute-done.1 = bf16[1024,4000]{0,1:T(8,128)(2,1)} collective-permute-done((bf16[1024,4000]{0,1:T(8,128)(2,1)S(1)}, bf16[1024,4000]{0,1:T(8,128)(2,1)}, u32[]{:S(2)}, u32[]{:S(2)}) %collective-permute-start.1) | collective-permute-done | bytes 8192032 | tf_op jit(solution)/shard_map/ppermute | solution.py:45
  676.6 178.3 %all-reduce = f32[1024]{0:T(1024)S(1)} all-reduce(f32[1024]{0:T(1024)S(1)} %get-tuple-element.21), channel_id=4, replica_groups=mesh['teacher'=4,'vocab'=8] {'teacher'}, use_global_device_ids=true, to_apply=%region_7.0.clone | all-reduce | flops 1024 | bytes 8192
  854.9 7.4 constant_dynamic-update-slice_fusion.7
  862.4 7.6 constant_dynamic-update-slice_fusion.6
  870.0 7.6 constant_dynamic-update-slice_fusion.5
  881.7 7.4 constant_dynamic-update-slice_fusion.3
  889.2 7.4 constant_dynamic-update-slice_fusion.2
  896.6 7.4 constant_dynamic-update-slice_fusion.1
  908.1 17.1 %fusion.4 = f32[4000,256]{1,0:T(8,128)} fusion(bf16[256,4096]{1,0:T(8,128)(2,1)} %param.6, bf16[8192,4000]{0,1:T(8,128)(2,1)} %constant_dynamic-update-slice_fusion, s32[]{:T(128)S(6)} %select_n.14), kind=kOutput, calls=%fused_computation.4 | convolution fusion | flops 8388608000 | bytes 38961156 | tf_op jit(solution)/shard_map/dot_general | solution.py:51
  930.4 13.6 %pmax.15 = f32[2,256]{1,0:T(2,128)S(1)} all-reduce(f32[2,256]{1,0:T(2,128)S(1)} %fusion.8), channel_id=1, replica_groups=mesh['teacher'=4,'vocab'=8] {'vocab'}, use_global_device_ids=true, to_apply=%region_9.10 | all-reduce | flops 512 | bytes 4096 | tf_op jit(solution)/shard_map/pmax | solution.py:21
  947.9 13.9 %psum.30 = f32[2,256]{1,0:T(2,128)S(1)} all-reduce(f32[2,256]{1,0:T(2,128)S(1)} %exponential_reduce_fusion), channel_id=1, replica_groups=mesh['teacher'=4,'vocab'=8] {'vocab'}, use_global_device_ids=true, to_apply=%region_11.12 | all-reduce | flops 512 | bytes 4096 | tf_op jit(solution)/shard_map/psum | solution.py:22
  961.8 5.6 subtract_convert_fusion
  967.4 18.1 %fusion.2 = f32[4096,256]{1,0:T(8,128)} fusion(bf16[256,4000]{0,1:T(8,128)(2,1)S(1)} %get-tuple-element.19, bf16[8192,4000]{0,1:T(8,128)(2,1)} %constant_dynamic-update-slice_fusion, s32[]{:T(128)S(6)} %select_n.14), kind=kOutput, calls=%fused_computation.2 | convolution fusion | flops 8388608000 | bytes 39010308 | tf_op jit(solution)/shard_map/dot_general | solution.py:60
  990.2 29.0 %all_to_all.19 = bf16[256,4,1024]{0,2,1:T(8,128)(2,1)S(1)} all-to-all(bf16[256,4,1024]{0,2,1:T(8,128)(2,1)} %bitcast.38), channel_id=1, replica_groups=mesh['teacher'=4,'vocab'=8] {'teacher'}, dimensions={1} | all-to-all | bytes 4194304 | tf_op jit(solution)/shard_map/all_to_all | solution.py:67
  1021.8 37.6 %psum.31 = f32[]{:T(128)} all-reduce(f32[]{:T(128)} %get-tuple-element.20), channel_id=1, replica_groups=mesh['teacher'=4,'vocab'=8] {'teacher','vocab'}, use_global_device_ids=true, to_apply=%region_13.14 | all-reduce | flops 1 | bytes 8 | tf_op jit(solution)/shard_map/psum | solution.py:57
  1062.1 58.4 %all-gather.4.cloned.1.call-done = bf16[1024,4000]{0,1:T(8,128)(2,1)} async-done(((bf16[256,4000]{0,1:T(8,128)(2,1)}), bf16[1024,4000]{0,1:T(8,128)(2,1)}) %all-gather.4.cloned.1.call-update) | async-done | bytes 8192016 | tf_op jit(solution)/shard_map/all_gather | solution.py:68
  1120.5 15.9 %convolution_bitcast_fusion = f32[1024,4000]{0,1:T(8,128)} fusion(bf16[1024,4000]{0,1:T(8,128)(2,1)} %all-gather.4.cloned.1.call-done, bf16[1024,1024]{1,0:T(8,128)(2,1)} %bitcast.39), kind=kOutput, calls=%fused_computation.10 | convolution fusion | flops 8388608000 | bytes 26673152 | tf_op jit(solution)/shard_map/dot_general | solution.py:69
  (42 shorter events, 33.9 us)
Async XLA Ops:
  7.2 87.2 %all-gather.6.cloned.1.call-start = ((), (), s32[]{:S(2)}) async-start(), calls=%async_computation.6 | async-start | bytes 9437184 | tf_op jit(solution)/shard_map/all_gather | solution.py:29
  7.9 917.3 %reduce-scatter.3.cloned.1.call-start = ((), (), s32[]{:S(2)}) async-start(), calls=%async_computation.3 | async-start | bytes 20480000 | tf_op jit(solution)/shard_map/reduce_scatter | solution.py:39
  183.2 492.1 %copy-start.4 = (u32[32]{0:T(128)S(1)}, u32[32]{0:T(128)}, u32[]{:S(2)}) copy-start(u32[32]{0:T(128)} %constant.42) | copy-start | bytes 388
  183.3 876.8 %reduce-scatter.5.cloned.1.call-start = ((), (), s32[]{:S(2)}) async-start(), calls=%async_computation.4 | async-start | bytes 4718592 | tf_op jit(solution)/shard_map/reduce_scatter | solution.py:59
  183.3 310.7 %collective-permute-start = (bf16[1024,4000]{0,1:T(8,128)(2,1)}, bf16[1024,4000]{0,1:T(8,128)(2,1)S(1)}, u32[]{:S(2)}, u32[]{:S(2)}) collective-permute-start(bf16[1024,4000]{0,1:T(8,128)(2,1)} %param.7), channel_id=1, source_target_pairs={{0,8},{8,16},{16,24},{24,0},{1,9},{9,17},{17,25},{25,1},{2,10},{10... | collective-permute-start | bytes 24576008 | tf_op jit(solution)/shard_map/ppermute | solution.py:45
  494.0 3.3 copy-start.2
  497.3 178.0 %collective-permute-start.1 = (bf16[1024,4000]{0,1:T(8,128)(2,1)S(1)}, bf16[1024,4000]{0,1:T(8,128)(2,1)}, u32[]{:S(2)}, u32[]{:S(2)}) collective-permute-start(bf16[1024,4000]{0,1:T(8,128)(2,1)S(1)} %collective-permute-done), channel_id=1, source_target_pairs={{0,8},{8,16},{16,24},{24,0},{1,9},{9,17},{17,25},{25,1},{2,10},{10... | collective-permute-start | bytes 24576008 | tf_op jit(solution)/shard_map/ppermute | solution.py:45
  675.3 179.6 %collective-permute-start.2 = (bf16[1024,4000]{0,1:T(8,128)(2,1)}, bf16[1024,4000]{0,1:T(8,128)(2,1)}, u32[]{:S(2)}, u32[]{:S(2)}) collective-permute-start(bf16[1024,4000]{0,1:T(8,128)(2,1)} %collective-permute-done.1), channel_id=1, source_target_pairs={{0,8},{8,16},{16,24},{24,0},{1,9},{9,17},{17,25},{25,1},{2,10},{10... | collective-permute-start | bytes 24576008 | tf_op jit(solution)/shard_map/ppermute | solution.py:45
  862.4 15.2 %slice-start = ((s8[8192000]{0:T(1024)(128)(4,1)}), s8[4194304]{0:T(1024)(128)(4,1)S(1)}, s32[]{:S(2)}) async-start(s8[8192000]{0:T(1024)(128)(4,1)} %bitcast.35), calls=%async_computation.7 | async-start | bytes 8388608
  870.0 7.6 slice-start.1
  925.2 4.6 copy-start.1
  927.8 2.0 copy-start
  967.4 18.1 %copy-start.3 = (bf16[256,4000]{0,1:T(8,128)(2,1)}, bf16[256,4000]{0,1:T(8,128)(2,1)S(1)}, u32[]{:S(2)}) copy-start(bf16[256,4000]{0,1:T(8,128)(2,1)S(1)} %get-tuple-element.19) | copy-start | bytes 6144004
  985.6 134.9 %all-gather.4.cloned.1.call-start = ((), (), s32[]{:S(2)}) async-start(), calls=%async_computation.5 | async-start | bytes 10240000 | tf_op jit(solution)/shard_map/all_gather | solution.py:68
Sparse Core Ops, SparseCore 0:
  9.6 84.7 all-gather.5
  183.4 281.6 reduce-scatter.2
  985.7 48.3 reduce-scatter.4
  1035.9 84.5 all-gather.3
